TPU v7x, 512 devices: a whole 4x8x8 slice. The times are simulated.
512 devices in a mesh: grp: 8 (over x, core), blk: 64 (over y, z).
Axes of the slice: x: 4, y: 8, z: 8, core: 2. Of those that a mesh axis runs over, the one named last changes fastest.
Arguments:
- features: bfloat16 [65536, 256], P(('grp', 'blk')), may hold values from -6 to 6
- dest: int32 [65536, 1], P(('grp', 'blk')), may hold values from 0 to 63; in each aligned block of 128 rows (0 to 127, 128 to 255, ...) at most 4 rows name the same one
- placement: int32 [512, 256], P(('grp', 'blk')), may hold values from 0 to 255, each once within a row
- weight: bfloat16 [27, 256, 128], replicated, may hold values from -0.078125 to 0.078125
- grad_out: bfloat16 [64, 512, 4, 128], P('grp', 'blk'), may hold values from -6 to 6
Outputs:
- output: bfloat16 [64, 512, 4, 128], P('grp', 'blk')
- grad_rows: bfloat16 [65536, 256], P(('grp', 'blk'))
- weight_grad: bfloat16 [27, 256, 128], replicated
Inputs may be any that keep to these rules, and one draw needn't show every extreme that they name: `dest`: among the rows of one device no value is named by more than 4 rows, a bound that some block reaches. `placement`: each row is a permutation of 0 to 255.
All inputs are finite; a program needn't handle non-finite values.
Results may differ from a plain program's by a relative error of at most 0.0013.
Values may be sent and summed in bfloat16 or wider, within the bound.
A program may use at most 64 MiB of HBM per device.

v0:
```python
import math
import jax
import jax.numpy as jnp
from jax import lax
from jax.sharding import PartitionSpec as P


def extended(cells, sides, width):
    for axis, dim in sides:
        count = lax.axis_size(axis)
        ends = count - 1
        head = lax.slice_in_dim(cells, 0, width, axis=dim)
        tail = lax.slice_in_dim(cells, cells.shape[dim] - width, cells.shape[dim], axis=dim)
        cells = jnp.concatenate(
            [
                lax.ppermute(tail, axis, [(i, (i + 1) % count) for i in range(ends)]),
                cells,
                lax.ppermute(head, axis, [((i + 1) % count, i) for i in range(ends)]),
            ],
            axis=dim,
        )
    return cells


def shards(features, dest, placement, weight, grad_out):
    row_count, channels = features.shape
    blk_count = lax.axis_size("blk")
    grp_count = lax.axis_size("grp")
    voxel_of_slot = placement[0]
    voxel_count = voxel_of_slot.shape[0]
    capacity = voxel_count // blk_count
    size_x, size_y, size_z, out_channels = grad_out.shape
    target = dest[:, 0]
    owners = jnp.arange(blk_count, dtype=jnp.int32)
    one_hot = (target[:, None] == owners[None, :]).astype(jnp.int32)
    slot_rank = jnp.sum((jnp.cumsum(one_hot, axis=0) - one_hot) * one_hot, axis=1)
    send_counts = jnp.sum(one_hot, axis=0).reshape(blk_count, 1)
    slot_index = target * capacity + slot_rank
    outgoing = jnp.zeros((voxel_count, channels), jnp.bfloat16).at[slot_index].set(features)
    incoming, recv_counts = (
        lax.all_to_all(
            outgoing.reshape(blk_count, capacity, channels),
            "blk",
            split_axis=0,
            concat_axis=0,
            tiled=True,
        ),
        lax.all_to_all(send_counts, "blk", split_axis=0, concat_axis=0, tiled=True),
    )
    filled = (
        (jnp.arange(capacity, dtype=jnp.int32)[None, :] < recv_counts)
        .reshape(-1)
        .astype(jnp.float32)
    )
    voxel_rows = (
        jnp.zeros((voxel_count, channels), jnp.bfloat16)
        .at[voxel_of_slot]
        .set(incoming.reshape(voxel_count, channels))
    )
    occupied = jnp.zeros((voxel_count,), jnp.float32).at[voxel_of_slot].set(filled)[:, None]
    voxel_grid = voxel_rows.reshape(size_x, size_y, size_z, channels)
    padded = extended(voxel_grid, (("grp", 0), ("blk", 1)), 1)
    padded = jnp.pad(padded, ((0, 0), (0, 0), (1, 1), (0, 0)))
    shifted = []
    total = jnp.zeros((voxel_count, out_channels), jnp.float32)
    for offset in range(27):
        shift_x, shift_y, shift_z = (offset // 9, offset // 3 % 3, offset % 3)
        window = padded[
            shift_x : shift_x + size_x, shift_y : shift_y + size_y, shift_z : shift_z + size_z
        ].reshape(voxel_count, channels)
        shifted.append(window)
        total = total + jnp.dot(window, weight[offset], preferred_element_type=jnp.float32)
    output = (total * occupied).astype(jnp.bfloat16).reshape(size_x, size_y, size_z, out_channels)
    masked_grad = (
        grad_out.reshape(voxel_count, out_channels).astype(jnp.float32) * occupied
    ).astype(jnp.bfloat16)
    grad_padded = extended(
        masked_grad.reshape(size_x, size_y, size_z, out_channels), (("grp", 0), ("blk", 1)), 1
    )
    grad_padded = jnp.pad(grad_padded, ((0, 0), (0, 0), (1, 1), (0, 0)))
    back_total = jnp.zeros((voxel_count, channels), jnp.float32)
    partials = []
    for offset in range(27):
        shift_x, shift_y, shift_z = (offset // 9, offset // 3 % 3, offset % 3)
        window = grad_padded[
            2 - shift_x : 2 - shift_x + size_x,
            2 - shift_y : 2 - shift_y + size_y,
            2 - shift_z : 2 - shift_z + size_z,
        ].reshape(voxel_count, out_channels)
        back_total = back_total + lax.dot_general(
            window, weight[offset], (((1,), (1,)), ((), ())), preferred_element_type=jnp.float32
        )
        partials.append(
            lax.dot_general(
                shifted[offset],
                masked_grad,
                (((0,), (0,)), ((), ())),
                preferred_element_type=jnp.float32,
            )
        )
    grad_grid = (back_total * occupied).astype(jnp.bfloat16)
    weight_terms = jnp.stack(partials).reshape(27 * channels, out_channels)
    grad_scale = 1.0 / math.sqrt(row_count * blk_count * grp_count)
    weight_grad = (lax.psum(weight_terms, ("grp", "blk")) * grad_scale).astype(jnp.bfloat16)
    weight_grad = weight_grad.reshape(27, channels, out_channels)
    returning = grad_grid[voxel_of_slot].reshape(blk_count, capacity, channels)
    returned = lax.all_to_all(returning, "blk", split_axis=0, concat_axis=0, tiled=True)
    grad_rows = returned.reshape(voxel_count, channels)[slot_index]
    return (output, grad_rows, weight_grad)


def solution(mesh):
    in_specs = (
        P(("grp", "blk"), None),
        P(("grp", "blk"), None),
        P(("grp", "blk"), None),
        P(),
        P("grp", "blk", None, None),
    )
    out_specs = (P("grp", "blk", None, None), P(("grp", "blk"), None), P())
    return jax.shard_map(shards, mesh=mesh, in_specs=in_specs, out_specs=out_specs, check_vma=False)
```

profile of v0, /device:TPU:24, one launch (start us, length us, event | category | flops | bytes accessed | tf_op | source)
XLA Modules:
  0.0 480.3 jit_solution(8768574311076272875)
XLA Ops:
  9.6 16.4 %all-to-all-start.1 = ((s32[64,1,1]{2,1,0:T(1,128)}), s32[64,1,1]{2,1,0:T(1,128)S(1)}, u32[]{:S(2)}, u32[]{:S(2)}) async-start(s32[64,1,1]{2,1,0:T(1,128)} %copy.183), calls=%async_computation.1 | async-start | bytes 65536 | tf_op jit(solution)/shard_map/all_to_all | solution.py:48
  29.5 5.8 %all-to-all-done.1 = s32[64,1,1]{2,1,0:T(1,128)S(1)} async-done(((s32[64,1,1]{2,1,0:T(1,128)}), s32[64,1,1]{2,1,0:T(1,128)S(1)}, u32[]{:S(2)}, u32[]{:S(2)}) %all-to-all-start.1) | async-done | bytes 288 | tf_op jit(solution)/shard_map/all_to_all | solution.py:48
  35.3 7.3 %all-to-all-start = ((bf16[64,4,256]{2,1,0:T(4,128)(2,1)}), bf16[64,4,256]{2,1,0:T(4,128)(2,1)S(1)}, u32[]{:S(2)}, u32[]{:S(2)}) async-start(bf16[64,4,256]{2,1,0:T(4,128)(2,1)} %reshape.379), calls=%async_computation | async-start | bytes 262144 | tf_op jit(solution)/shard_map/all_to_all | solution.py:41
  47.8 3.0 collective-permute-start.4
  51.8 3.4 collective-permute-start.6
  55.2 4.6 collective-permute-start.7
  68.6 1.9 collective-permute-start
  72.5 12.3 %all-to-all-start.2 = ((bf16[64,4,256]{2,1,0:T(4,128)(2,1)}), bf16[64,4,256]{2,1,0:T(4,128)(2,1)S(1)}, u32[]{:S(2)}, u32[]{:S(2)}) async-start(bf16[64,4,256]{2,1,0:T(4,128)(2,1)} %reshape.436), calls=%async_computation.2 | async-start | bytes 262144 | tf_op jit(solution)/shard_map/all_to_all | solution.py:107
  86.4 4.1 collective-permute-done.1
  90.6 3.4 collective-permute-start.2
  93.9 4.8 collective-permute-start.3
  119.0 1.6 copy.176
  122.2 1.6 copy.175
  125.4 1.6 copy.173
  128.6 1.6 copy.172
  131.8 1.6 copy.170
  133.4 1.6 reshape.396
  135.0 1.6 copy.169
  138.2 1.6 copy.168
  141.4 1.6 copy.167
  143.0 1.6 reshape.393
  144.6 1.6 copy.165
  147.8 1.6 copy.164
  151.0 1.6 copy.162
  154.9 1.6 reshape.387
  156.5 1.6 copy.158
  159.7 1.6 copy.157
  161.3 1.6 reshape.384
  163.0 1.6 copy.155
  182.7 1.8 copy-done.2
  188.6 281.5 %all-reduce.4.cloned.1.call-done = f32[6912,128]{1,0:T(8,128)} async-done(((f32[6912,128]{1,0:T(8,128)}), f32[6912,128]{1,0:T(8,128)}) %all-reduce.4.cloned.1.call-update) | async-done | bytes 3538960 | tf_op jit(solution)/shard_map/psum | solution.py:104
  470.1 3.4 multiply_convert_fusion
  (238 shorter events, 82.6 us)
Async XLA Ops:
  9.6 25.6 %all-to-all-start.1 = ((s32[64,1,1]{2,1,0:T(1,128)}), s32[64,1,1]{2,1,0:T(1,128)S(1)}, u32[]{:S(2)}, u32[]{:S(2)}) async-start(s32[64,1,1]{2,1,0:T(1,128)} %copy.183), calls=%async_computation.1 | async-start | bytes 65536 | tf_op jit(solution)/shard_map/all_to_all | solution.py:48
  35.3 31.7 %all-to-all-start = ((bf16[64,4,256]{2,1,0:T(4,128)(2,1)}), bf16[64,4,256]{2,1,0:T(4,128)(2,1)S(1)}, u32[]{:S(2)}, u32[]{:S(2)}) async-start(bf16[64,4,256]{2,1,0:T(4,128)(2,1)} %reshape.379), calls=%async_computation | async-start | bytes 262144 | tf_op jit(solution)/shard_map/all_to_all | solution.py:41
  42.6 19.2 %copy-start = (bf16[27,256,128]{2,1,0:T(8,128)(2,1)S(1)}, bf16[27,256,128]{2,1,0:T(8,128)(2,1)}, u32[]{:S(2)}) copy-start(bf16[27,256,128]{2,1,0:T(8,128)(2,1)} %param.8) | copy-start | bytes 5308420
  46.5 5.3 %collective-permute-start.5 = (bf16[1,8,4,128]{3,2,1,0:T(4,128)(2,1)S(1)}, bf16[1,8,4,128]{3,2,1,0:T(4,128)(2,1)S(1)}, u32[]{:S(2)}, u32[]{:S(2)}) collective-permute-start(bf16[1,8,4,128]{3,2,1,0:T(4,128)(2,1)S(1)} %bitcast.495), channel_id=1, source_target_pairs={{64,0},{128,64},{192,128},{256,192},{320,256},{384,320},{448,384},... | collective-permute-start | bytes 24584 | tf_op jit(solution)/shard_map/ppermute | solution.py:18
  47.8 4.0 collective-permute-start.4
  51.8 8.0 %collective-permute-start.6 = (bf16[10,1,4,128]{3,2,1,0:T(4,128)(2,1)S(1)}, bf16[10,1,4,128]{3,2,1,0:T(4,128)(2,1)S(1)}, u32[]{:S(2)}, u32[]{:S(2)}) collective-permute-start(bf16[10,1,4,128]{3,2,1,0:T(4,128)(2,1)S(1)} %get-tuple-element.65), channel_id=1, source_target_pairs={{0,1},{1,2},{2,3},{3,4},{4,5},{5,6},{6,7},{7,8},{8,9},{9,10},{10,1... | collective-permute-start | bytes 30728 | tf_op jit(solution)/shard_map/ppermute | solution.py:16
  55.2 5.9 %collective-permute-start.7 = (bf16[10,1,4,128]{3,2,1,0:T(4,128)(2,1)S(1)}, bf16[10,1,4,128]{3,2,1,0:T(4,128)(2,1)S(1)}, u32[]{:S(2)}, u32[]{:S(2)}) collective-permute-start(bf16[10,1,4,128]{3,2,1,0:T(4,128)(2,1)S(1)} %get-tuple-element.66), channel_id=1, source_target_pairs={{1,0},{2,1},{3,2},{4,3},{5,4},{6,5},{7,6},{8,7},{9,8},{10,9},{11,1... | collective-permute-start | bytes 30728 | tf_op jit(solution)/shard_map/ppermute | solution.py:18
  68.6 17.7 %collective-permute-start = (bf16[1,8,4,256]{3,1,2,0:T(8,128)(2,1)S(1)}, bf16[1,8,4,256]{3,1,2,0:T(8,128)(2,1)S(1)}, u32[]{:S(2)}, u32[]{:S(2)}) collective-permute-start(bf16[1,8,4,256]{3,1,2,0:T(8,128)(2,1)S(1)} %copy.152), channel_id=1, source_target_pairs={{0,64},{64,128},{128,192},{192,256},{256,320},{320,384},{384,448},... | collective-permute-start | bytes 49160 | tf_op jit(solution)/shard_map/ppermute | solution.py:16
  72.5 27.1 %all-to-all-start.2 = ((bf16[64,4,256]{2,1,0:T(4,128)(2,1)}), bf16[64,4,256]{2,1,0:T(4,128)(2,1)S(1)}, u32[]{:S(2)}, u32[]{:S(2)}) async-start(bf16[64,4,256]{2,1,0:T(4,128)(2,1)} %reshape.436), calls=%async_computation.2 | async-start | bytes 262144 | tf_op jit(solution)/shard_map/all_to_all | solution.py:107
  84.9 385.2 %all-reduce.4.cloned.1.call-start = ((), (), s32[]{:S(2)}) async-start(), calls=%async_computation.3 | async-start | bytes 7077888 | tf_op jit(solution)/shard_map/psum | solution.py:104
  85.0 13.8 %copy-start.18 = (bf16[8,8,4,256]{3,2,1,0:T(4,128)(2,1)}, bf16[8,8,4,256]{3,2,1,0:T(4,128)(2,1)S(1)}, u32[]{:S(2)}) copy-start(bf16[8,8,4,256]{3,2,1,0:T(4,128)(2,1)S(1)} %reshape.381) | copy-start | bytes 393220
  85.0 5.5 %collective-permute-start.1 = (bf16[1,8,4,256]{3,1,2,0:T(8,128)(2,1)S(1)}, bf16[1,8,4,256]{3,1,2,0:T(8,128)(2,1)S(1)}, u32[]{:S(2)}, u32[]{:S(2)}) collective-permute-start(bf16[1,8,4,256]{3,1,2,0:T(8,128)(2,1)S(1)} %copy.153), channel_id=1, source_target_pairs={{64,0},{128,64},{192,128},{256,192},{320,256},{384,320},{448,384},... | collective-permute-start | bytes 49160 | tf_op jit(solution)/shard_map/ppermute | solution.py:18
  86.4 14.8 %copy-start.31 = (bf16[9,8,4,256]{3,1,2,0:T(8,128)(2,1)}, bf16[9,8,4,256]{3,1,2,0:T(8,128)(2,1)S(1)}, u32[]{:S(2)}) copy-start(bf16[9,8,4,256]{3,1,2,0:T(8,128)(2,1)S(1)} %get-tuple-element.53) | copy-start | bytes 442372
  90.5 8.3 %copy-start.27 = (bf16[9,8,4,256]{3,1,2,0:T(8,128)(2,1)}, bf16[9,8,4,256]{3,1,2,0:T(8,128)(2,1)S(1)}, u32[]{:S(2)}) copy-start(bf16[9,8,4,256]{3,1,2,0:T(8,128)(2,1)S(1)} %get-tuple-element.71) | copy-start | bytes 442372
  90.6 10.6 %collective-permute-start.2 = (bf16[10,1,4,256]{3,1,2,0:T(2,128)(2,1)S(1)}, bf16[10,1,4,256]{3,1,2,0:T(2,128)(2,1)S(1)}, u32[]{:S(2)}, u32[]{:S(2)}) collective-permute-start(bf16[10,1,4,256]{3,1,2,0:T(2,128)(2,1)S(1)} %get-tuple-element.50), channel_id=1, source_target_pairs={{0,1},{1,2},{2,3},{3,4},{4,5},{5,6},{6,7},{7,8},{8,9},{9,10},{10,1... | collective-permute-start | bytes 61448 | tf_op jit(solution)/shard_map/ppermute | solution.py:16
  93.9 7.2 %collective-permute-start.3 = (bf16[10,1,4,256]{3,1,2,0:T(2,128)(2,1)S(1)}, bf16[10,1,4,256]{3,1,2,0:T(2,128)(2,1)S(1)}, u32[]{:S(2)}, u32[]{:S(2)}) collective-permute-start(bf16[10,1,4,256]{3,1,2,0:T(2,128)(2,1)S(1)} %get-tuple-element.51), channel_id=1, source_target_pairs={{1,0},{2,1},{3,2},{4,3},{5,4},{6,5},{7,6},{8,7},{9,8},{10,9},{11,1... | collective-permute-start | bytes 61448 | tf_op jit(solution)/shard_map/ppermute | solution.py:18
  105.5 1.8 copy-start.20
  154.9 15.8 %copy-start.8 = (bf16[256,256]{1,0:T(8,128)(2,1)S(1)}, bf16[256,256]{1,0:T(8,128)(2,1)}, u32[]{:S(2)}) copy-start(bf16[256,256]{1,0:T(8,128)(2,1)} %reshape.386) | copy-start | bytes 393220
  166.2 4.7 copy-start.17
  166.2 4.9 %copy-start.16 = (bf16[256,256]{1,0:T(8,128)(2,1)S(1)}, bf16[256,256]{1,0:T(8,128)(2,1)}, u32[]{:S(2)}) copy-start(bf16[256,256]{1,0:T(8,128)(2,1)} %reshape.388) | copy-start | bytes 393220
  166.2 5.1 %copy-start.11 = (bf16[256,256]{1,0:T(8,128)(2,1)S(1)}, bf16[256,256]{1,0:T(8,128)(2,1)}, u32[]{:S(2)}) copy-start(bf16[256,256]{1,0:T(8,128)(2,1)} %reshape.389) | copy-start | bytes 393220
  166.2 5.3 %copy-start.15 = (bf16[256,256]{1,0:T(8,128)(2,1)S(1)}, bf16[256,256]{1,0:T(8,128)(2,1)}, u32[]{:S(2)}) copy-start(bf16[256,256]{1,0:T(8,128)(2,1)} %reshape.390) | copy-start | bytes 393220
  167.3 4.3 copy-start.14
  168.4 3.4 copy-start.10
  169.5 2.5 copy-start.13
  170.7 1.5 copy-start.12
  170.9 1.7 copy-start.26
  171.1 2.0 copy-start.1
  182.7 1.8 copy-start.2
  184.5 1.4 copy-start.6
  185.4 1.3 copy-start.4
  185.4 1.5 copy-start.3
  (13 other events, 11.8 us)
Sparse Core Ops, SparseCore 0:
  184.6 285.4 all-reduce.3
where the time goes:
time: 482 us; the launch traced here: 480 us
  waiting for transfers between devices  293 us (61%)
  local copies, waits for them, and re-layouts  80.7 us (17%)
  starting transfers between devices  59.6 us (12%)
  matrix products  20.7 us (4%)
  between operations  15.2 us (3%)
  other arithmetic  11.4 us (2%)
    psum x1, waiting for transfers between devices, shards(): lax.psum(weight_terms, ('grp', 'blk')) * grad_scale  282 us
    slice x29, local copies, waits for them, and re-layouts, shards(): padded[shift_x:shift_x + size_x, shift_y:shift_y + size_y, shift_z:shift_...  32.4 us
    reshape x26, local copies, waits for them, and re-layouts, shards(): window = padded[shift_x:shift_x + size_x, shift_y:shift_y + size_y, shift...  30.6 us
    all_to_all x1, starting transfers between devices, shards(): lax.all_to_all(send_counts, 'blk', split_axis=0, concat_axis=0, tiled=True)  16.4 us
    all_to_all x1, starting transfers between devices, shards(): lax.all_to_all(returning, 'blk', split_axis=0, concat_axis=0, tiled=True)  12.3 us
    ppermute x4, starting transfers between devices, extended(): lax.ppermute(head, axis, [((i + 1) % count, i) for i in range(ends)])  11.9 us
    ppermute x4, starting transfers between devices, extended(): lax.ppermute(tail, axis, [(i, (i + 1) % count) for i in range(ends)])  11.7 us
  transfers between devices with their start and end apart: 12, of which 4 were waited for; matrix products, arithmetic and copies ran while one was open for 4% of the time, Pallas kernels for 0%

commit v1 on v0

--- a/solution.py
+++ b/solution.py
@@ -101,7 +101,7 @@
     grad_grid = (back_total * occupied).astype(jnp.bfloat16)
     weight_terms = jnp.stack(partials).reshape(27 * channels, out_channels)
     grad_scale = 1.0 / math.sqrt(row_count * blk_count * grp_count)
-    weight_grad = (lax.psum(weight_terms, ("grp", "blk")) * grad_scale).astype(jnp.bfloat16)
+    weight_grad = (lax.psum(lax.psum(weight_terms, "blk"), "grp") * grad_scale).astype(jnp.bfloat16)
     weight_grad = weight_grad.reshape(27, channels, out_channels)
     returning = grad_grid[voxel_of_slot].reshape(blk_count, capacity, channels)
     returned = lax.all_to_all(returning, "blk", split_axis=0, concat_axis=0, tiled=True)

time: 482 us -> 402 us (0.83)
  the two profiles are of different devices: /device:TPU:24 before, /device:TPU:8 now
where the time goes in v1:
time: 402 us; the launch traced here: 401 us
  waiting for transfers between devices  209 us (52%)
  local copies, waits for them, and re-layouts  69.7 us (17%)
  starting transfers between devices  58.1 us (14%)
  matrix products  38.3 us (10%)
  between operations  15.1 us (4%)
  other arithmetic  11.3 us (3%)
    psum x1, waiting for transfers between devices, shards(): lax.psum(weight_terms, 'blk')  119 us
    psum x1, waiting for transfers between devices, shards(): lax.psum(lax.psum(weight_terms, 'blk'), 'grp') * grad_scale  76.8 us
    reshape x26, local copies, waits for them, and re-layouts, shards(): window = padded[shift_x:shift_x + size_x, shift_y:shift_y + size_y, shift...  31.9 us
    dot_general x27, matrix products, shards(): lax.dot_general(shifted[offset], masked_grad, (((0,), (0,)), ((), ())), p...  24.7 us
    slice x29, local copies, waits for them, and re-layouts, shards(): padded[shift_x:shift_x + size_x, shift_y:shift_y + size_y, shift_z:shift_...  23.9 us
    all_to_all x1, starting transfers between devices, shards(): lax.all_to_all(send_counts, 'blk', split_axis=0, concat_axis=0, tiled=True)  16.6 us
    all_to_all x1, starting transfers between devices, shards(): lax.all_to_all(returning, 'blk', split_axis=0, concat_axis=0, tiled=True)  12.4 us
    ppermute x4, starting transfers between devices, extended(): lax.ppermute(head, axis, [((i + 1) % count, i) for i in range(ends)])  11.9 us
  transfers between devices with their start and end apart: 13, of which 5 were waited for; matrix products, arithmetic and copies ran while one was open for 17% of the time, Pallas kernels for 0%

profile of v1, /device:TPU:8, one launch (start us, length us, event | category | flops | bytes accessed | tf_op | source)
XLA Modules:
  0.0 401.1 jit_solution(11206996014002651126)
XLA Ops:
  9.6 16.6 %all-to-all-start.1 = ((s32[64,1,1]{2,1,0:T(1,128)}), s32[64,1,1]{2,1,0:T(1,128)S(1)}, u32[]{:S(2)}, u32[]{:S(2)}) async-start(s32[64,1,1]{2,1,0:T(1,128)} %copy.183), calls=%async_computation.1 | async-start | bytes 65536 | tf_op jit(solution)/shard_map/all_to_all | solution.py:48
  29.7 7.5 %all-to-all-done.1 = s32[64,1,1]{2,1,0:T(1,128)S(1)} async-done(((s32[64,1,1]{2,1,0:T(1,128)}), s32[64,1,1]{2,1,0:T(1,128)S(1)}, u32[]{:S(2)}, u32[]{:S(2)}) %all-to-all-start.1) | async-done | bytes 288 | tf_op jit(solution)/shard_map/all_to_all | solution.py:48
  37.2 5.5 %all-to-all-start = ((bf16[64,4,256]{2,1,0:T(4,128)(2,1)}), bf16[64,4,256]{2,1,0:T(4,128)(2,1)S(1)}, u32[]{:S(2)}, u32[]{:S(2)}) async-start(bf16[64,4,256]{2,1,0:T(4,128)(2,1)} %reshape.379), calls=%async_computation | async-start | bytes 262144 | tf_op jit(solution)/shard_map/all_to_all | solution.py:41
  47.9 3.0 collective-permute-start.4
  51.9 3.4 collective-permute-start.6
  55.3 4.6 %collective-permute-start.7 = (bf16[10,1,4,128]{3,2,1,0:T(4,128)(2,1)S(1)}, bf16[10,1,4,128]{3,2,1,0:T(4,128)(2,1)S(1)}, u32[]{:S(2)}, u32[]{:S(2)}) collective-permute-start(bf16[10,1,4,128]{3,2,1,0:T(4,128)(2,1)S(1)} %get-tuple-element.66), channel_id=1, source_target_pairs={{1,0},{2,1},{3,2},{4,3},{5,4},{6,5},{7,6},{8,7},{9,8},{10,9},{11,1... | collective-permute-start | bytes 30728 | tf_op jit(solution)/shard_map/ppermute | solution.py:18
  68.7 1.9 collective-permute-start
  72.6 12.4 %all-to-all-start.2 = ((bf16[64,4,256]{2,1,0:T(4,128)(2,1)}), bf16[64,4,256]{2,1,0:T(4,128)(2,1)S(1)}, u32[]{:S(2)}, u32[]{:S(2)}) async-start(bf16[64,4,256]{2,1,0:T(4,128)(2,1)} %reshape.436), calls=%async_computation.2 | async-start | bytes 262144 | tf_op jit(solution)/shard_map/all_to_all | solution.py:107
  86.6 4.1 %collective-permute-done.1 = bf16[1,8,4,256]{3,1,2,0:T(8,128)(2,1)S(1)} collective-permute-done((bf16[1,8,4,256]{3,1,2,0:T(8,128)(2,1)S(1)}, bf16[1,8,4,256]{3,1,2,0:T(8,128)(2,1)S(1)}, u32[]{:S(2)}, u32[]{:S(2)}) %collective-permute-start.1) | collective-permute-done | bytes 16416 | tf_op jit(solution)/shard_map/ppermute | solution.py:18
  90.7 3.4 collective-permute-start.2
  94.1 4.8 %collective-permute-start.3 = (bf16[10,1,4,256]{3,1,2,0:T(2,128)(2,1)S(1)}, bf16[10,1,4,256]{3,1,2,0:T(2,128)(2,1)S(1)}, u32[]{:S(2)}, u32[]{:S(2)}) collective-permute-start(bf16[10,1,4,256]{3,1,2,0:T(2,128)(2,1)S(1)} %get-tuple-element.51), channel_id=1, source_target_pairs={{1,0},{2,1},{3,2},{4,3},{5,4},{6,5},{7,6},{8,7},{9,8},{10,9},{11,1... | collective-permute-start | bytes 61448 | tf_op jit(solution)/shard_map/ppermute | solution.py:18
  107.0 1.6 copy.158
  109.5 1.6 copy.157
  112.7 1.6 copy.155
  115.9 1.7 fusion.105
  117.7 1.8 fusion.29
  144.0 1.6 copy.163
  153.2 1.6 reshape.400
  155.6 1.7 reshape.407
  158.0 1.6 reshape.405
  160.3 1.6 reshape.404
  161.9 1.6 copy.176
  163.6 1.6 reshape.402
  165.2 1.6 copy.175
  166.8 1.6 reshape.401
  168.4 1.6 copy.173
  178.9 1.6 reshape.393
  182.9 1.6 reshape.390
  185.9 1.7 reshape.387
  192.1 118.8 %all-reduce.5.cloned.1.call-done = f32[6912,128]{1,0:T(8,128)} async-done(((f32[6912,128]{1,0:T(8,128)}), f32[6912,128]{1,0:T(8,128)}) %all-reduce.5.cloned.1.call-update) | async-done | bytes 3538960 | tf_op jit(solution)/shard_map/psum | solution.py:104
  314.1 76.8 %all-reduce.7.cloned.1.call-done = f32[6912,128]{1,0:T(8,128)} async-done(((f32[6912,128]{1,0:T(8,128)}), f32[6912,128]{1,0:T(8,128)}) %all-reduce.7.cloned.1.call-update) | async-done | bytes 3538960 | tf_op jit(solution)/shard_map/psum | solution.py:104
  390.9 3.4 multiply_convert_fusion
  (261 shorter events, 90.5 us)
Async XLA Ops:
  9.6 27.5 %all-to-all-start.1 = ((s32[64,1,1]{2,1,0:T(1,128)}), s32[64,1,1]{2,1,0:T(1,128)S(1)}, u32[]{:S(2)}, u32[]{:S(2)}) async-start(s32[64,1,1]{2,1,0:T(1,128)} %copy.183), calls=%async_computation.1 | async-start | bytes 65536 | tf_op jit(solution)/shard_map/all_to_all | solution.py:48
  37.2 30.0 %all-to-all-start = ((bf16[64,4,256]{2,1,0:T(4,128)(2,1)}), bf16[64,4,256]{2,1,0:T(4,128)(2,1)S(1)}, u32[]{:S(2)}, u32[]{:S(2)}) async-start(bf16[64,4,256]{2,1,0:T(4,128)(2,1)} %reshape.379), calls=%async_computation | async-start | bytes 262144 | tf_op jit(solution)/shard_map/all_to_all | solution.py:41
  42.7 19.1 %copy-start = (bf16[27,256,128]{2,1,0:T(8,128)(2,1)S(1)}, bf16[27,256,128]{2,1,0:T(8,128)(2,1)}, u32[]{:S(2)}) copy-start(bf16[27,256,128]{2,1,0:T(8,128)(2,1)} %param.8) | copy-start | bytes 5308420
  46.6 5.3 %collective-permute-start.5 = (bf16[1,8,4,128]{3,2,1,0:T(4,128)(2,1)S(1)}, bf16[1,8,4,128]{3,2,1,0:T(4,128)(2,1)S(1)}, u32[]{:S(2)}, u32[]{:S(2)}) collective-permute-start(bf16[1,8,4,128]{3,2,1,0:T(4,128)(2,1)S(1)} %bitcast.495), channel_id=1, source_target_pairs={{64,0},{128,64},{192,128},{256,192},{320,256},{384,320},{448,384},... | collective-permute-start | bytes 24584 | tf_op jit(solution)/shard_map/ppermute | solution.py:18
  47.9 4.0 %collective-permute-start.4 = (bf16[1,8,4,128]{3,2,1,0:T(4,128)(2,1)S(1)}, bf16[1,8,4,128]{3,2,1,0:T(4,128)(2,1)S(1)}, u32[]{:S(2)}, u32[]{:S(2)}) collective-permute-start(bf16[1,8,4,128]{3,2,1,0:T(4,128)(2,1)S(1)} %bitcast.494), channel_id=1, source_target_pairs={{0,64},{64,128},{128,192},{192,256},{256,320},{320,384},{384,448},... | collective-permute-start | bytes 24584 | tf_op jit(solution)/shard_map/ppermute | solution.py:16
  51.9 8.0 %collective-permute-start.6 = (bf16[10,1,4,128]{3,2,1,0:T(4,128)(2,1)S(1)}, bf16[10,1,4,128]{3,2,1,0:T(4,128)(2,1)S(1)}, u32[]{:S(2)}, u32[]{:S(2)}) collective-permute-start(bf16[10,1,4,128]{3,2,1,0:T(4,128)(2,1)S(1)} %get-tuple-element.65), channel_id=1, source_target_pairs={{0,1},{1,2},{2,3},{3,4},{4,5},{5,6},{6,7},{7,8},{8,9},{9,10},{10,1... | collective-permute-start | bytes 30728 | tf_op jit(solution)/shard_map/ppermute | solution.py:16
  55.3 5.9 %collective-permute-start.7 = (bf16[10,1,4,128]{3,2,1,0:T(4,128)(2,1)S(1)}, bf16[10,1,4,128]{3,2,1,0:T(4,128)(2,1)S(1)}, u32[]{:S(2)}, u32[]{:S(2)}) collective-permute-start(bf16[10,1,4,128]{3,2,1,0:T(4,128)(2,1)S(1)} %get-tuple-element.66), channel_id=1, source_target_pairs={{1,0},{2,1},{3,2},{4,3},{5,4},{6,5},{7,6},{8,7},{9,8},{10,9},{11,1... | collective-permute-start | bytes 30728 | tf_op jit(solution)/shard_map/ppermute | solution.py:18
  68.7 17.8 %collective-permute-start = (bf16[1,8,4,256]{3,1,2,0:T(8,128)(2,1)S(1)}, bf16[1,8,4,256]{3,1,2,0:T(8,128)(2,1)S(1)}, u32[]{:S(2)}, u32[]{:S(2)}) collective-permute-start(bf16[1,8,4,256]{3,1,2,0:T(8,128)(2,1)S(1)} %copy.152), channel_id=1, source_target_pairs={{0,64},{64,128},{128,192},{192,256},{256,320},{320,384},{384,448},... | collective-permute-start | bytes 49160 | tf_op jit(solution)/shard_map/ppermute | solution.py:16
  72.6 26.5 %all-to-all-start.2 = ((bf16[64,4,256]{2,1,0:T(4,128)(2,1)}), bf16[64,4,256]{2,1,0:T(4,128)(2,1)S(1)}, u32[]{:S(2)}, u32[]{:S(2)}) async-start(bf16[64,4,256]{2,1,0:T(4,128)(2,1)} %reshape.436), calls=%async_computation.2 | async-start | bytes 262144 | tf_op jit(solution)/shard_map/all_to_all | solution.py:107
  85.0 225.9 %all-reduce.5.cloned.1.call-start = ((), (), s32[]{:S(2)}) async-start(), calls=%async_computation.3 | async-start | bytes 7077888 | tf_op jit(solution)/shard_map/psum | solution.py:104
  85.1 13.8 %copy-start.24 = (bf16[8,8,4,256]{3,2,1,0:T(4,128)(2,1)}, bf16[8,8,4,256]{3,2,1,0:T(4,128)(2,1)S(1)}, u32[]{:S(2)}) copy-start(bf16[8,8,4,256]{3,2,1,0:T(4,128)(2,1)S(1)} %reshape.381) | copy-start | bytes 393220
  85.2 5.5 %collective-permute-start.1 = (bf16[1,8,4,256]{3,1,2,0:T(8,128)(2,1)S(1)}, bf16[1,8,4,256]{3,1,2,0:T(8,128)(2,1)S(1)}, u32[]{:S(2)}, u32[]{:S(2)}) collective-permute-start(bf16[1,8,4,256]{3,1,2,0:T(8,128)(2,1)S(1)} %copy.153), channel_id=1, source_target_pairs={{64,0},{128,64},{192,128},{256,192},{320,256},{384,320},{448,384},... | collective-permute-start | bytes 49160 | tf_op jit(solution)/shard_map/ppermute | solution.py:18
  86.5 14.1 %copy-start.41 = (bf16[9,8,4,256]{3,1,2,0:T(8,128)(2,1)}, bf16[9,8,4,256]{3,1,2,0:T(8,128)(2,1)S(1)}, u32[]{:S(2)}) copy-start(bf16[9,8,4,256]{3,1,2,0:T(8,128)(2,1)S(1)} %get-tuple-element.53) | copy-start | bytes 442372
  90.7 10.0 %copy-start.35 = (bf16[9,8,4,256]{3,1,2,0:T(8,128)(2,1)}, bf16[9,8,4,256]{3,1,2,0:T(8,128)(2,1)S(1)}, u32[]{:S(2)}) copy-start(bf16[9,8,4,256]{3,1,2,0:T(8,128)(2,1)S(1)} %get-tuple-element.71) | copy-start | bytes 442372
  90.7 9.9 %collective-permute-start.2 = (bf16[10,1,4,256]{3,1,2,0:T(2,128)(2,1)S(1)}, bf16[10,1,4,256]{3,1,2,0:T(2,128)(2,1)S(1)}, u32[]{:S(2)}, u32[]{:S(2)}) collective-permute-start(bf16[10,1,4,256]{3,1,2,0:T(2,128)(2,1)S(1)} %get-tuple-element.50), channel_id=1, source_target_pairs={{0,1},{1,2},{2,3},{3,4},{4,5},{5,6},{6,7},{7,8},{8,9},{9,10},{10,1... | collective-permute-start | bytes 61448 | tf_op jit(solution)/shard_map/ppermute | solution.py:16
  94.1 6.6 %collective-permute-start.3 = (bf16[10,1,4,256]{3,1,2,0:T(2,128)(2,1)S(1)}, bf16[10,1,4,256]{3,1,2,0:T(2,128)(2,1)S(1)}, u32[]{:S(2)}, u32[]{:S(2)}) collective-permute-start(bf16[10,1,4,256]{3,1,2,0:T(2,128)(2,1)S(1)} %get-tuple-element.51), channel_id=1, source_target_pairs={{1,0},{2,1},{3,2},{4,3},{5,4},{6,5},{7,6},{8,7},{9,8},{10,9},{11,1... | collective-permute-start | bytes 61448 | tf_op jit(solution)/shard_map/ppermute | solution.py:18
  122.1 1.8 copy-start.32
  141.6 249.3 %all-reduce.7.cloned.1.call-start = ((), (), s32[]{:S(2)}) async-start(), calls=%async_computation.4 | async-start | bytes 7077888 | tf_op jit(solution)/shard_map/psum | solution.py:104
  142.5 3.2 copy-start.31
  142.5 3.9 copy-start.29
  142.5 4.6 %copy-start.27 = (bf16[8,8,4,256]{3,1,2,0:T(8,128)(2,1)S(1)}, bf16[8,8,4,256]{3,1,2,0:T(8,128)(2,1)}, u32[]{:S(2)}) copy-start(bf16[8,8,4,256]{3,1,2,0:T(8,128)(2,1)} %get-tuple-element.49) | copy-start | bytes 393220
  142.7 12.2 %copy-start.8 = (bf16[8,8,4,256]{3,1,2,0:T(8,128)(2,1)S(1)}, bf16[8,8,4,256]{3,1,2,0:T(8,128)(2,1)}, u32[]{:S(2)}) copy-start(bf16[8,8,4,256]{3,1,2,0:T(8,128)(2,1)} %get-tuple-element.5) | copy-start | bytes 393220
  142.9 14.4 %copy-start.7 = (bf16[8,8,4,256]{3,1,2,0:T(8,128)(2,1)S(1)}, bf16[8,8,4,256]{3,1,2,0:T(8,128)(2,1)}, u32[]{:S(2)}) copy-start(bf16[8,8,4,256]{3,1,2,0:T(8,128)(2,1)} %get-tuple-element.6) | copy-start | bytes 393220
  144.0 15.6 %copy-start.5 = (bf16[8,8,4,256]{3,1,2,0:T(8,128)(2,1)S(1)}, bf16[8,8,4,256]{3,1,2,0:T(8,128)(2,1)}, u32[]{:S(2)}) copy-start(bf16[8,8,4,256]{3,1,2,0:T(8,128)(2,1)} %get-tuple-element.7) | copy-start | bytes 393220
  153.2 18.3 %copy-start.4 = (bf16[8,8,4,256]{3,1,2,0:T(8,128)(2,1)S(1)}, bf16[8,8,4,256]{3,1,2,0:T(8,128)(2,1)}, u32[]{:S(2)}) copy-start(bf16[8,8,4,256]{3,1,2,0:T(8,128)(2,1)} %get-tuple-element.11) | copy-start | bytes 393220
  155.6 17.6 %copy-start.3 = (bf16[8,8,4,256]{3,1,2,0:T(8,128)(2,1)S(1)}, bf16[8,8,4,256]{3,1,2,0:T(8,128)(2,1)}, u32[]{:S(2)}) copy-start(bf16[8,8,4,256]{3,1,2,0:T(8,128)(2,1)} %get-tuple-element.12) | copy-start | bytes 393220
  158.0 16.9 %copy-start.2 = (bf16[8,8,4,256]{3,1,2,0:T(8,128)(2,1)S(1)}, bf16[8,8,4,256]{3,1,2,0:T(8,128)(2,1)}, u32[]{:S(2)}) copy-start(bf16[8,8,4,256]{3,1,2,0:T(8,128)(2,1)} %get-tuple-element.13) | copy-start | bytes 393220
  160.3 16.2 %copy-start.1 = (bf16[8,8,4,256]{3,1,2,0:T(8,128)(2,1)S(1)}, bf16[8,8,4,256]{3,1,2,0:T(8,128)(2,1)}, u32[]{:S(2)}) copy-start(bf16[8,8,4,256]{3,1,2,0:T(8,128)(2,1)} %get-tuple-element.14) | copy-start | bytes 393220
  180.5 9.4 %copy-start.20 = (bf16[256,256]{1,0:T(8,128)(2,1)S(1)}, bf16[256,256]{1,0:T(8,128)(2,1)}, u32[]{:S(2)}) copy-start(bf16[256,256]{1,0:T(8,128)(2,1)} %reshape.389) | copy-start | bytes 393220
  184.5 6.0 %copy-start.17 = (bf16[256,256]{1,0:T(8,128)(2,1)S(1)}, bf16[256,256]{1,0:T(8,128)(2,1)}, u32[]{:S(2)}) copy-start(bf16[256,256]{1,0:T(8,128)(2,1)} %reshape.392) | copy-start | bytes 393220
  185.9 4.8 %copy-start.22 = (bf16[256,256]{1,0:T(8,128)(2,1)S(1)}, bf16[256,256]{1,0:T(8,128)(2,1)}, u32[]{:S(2)}) copy-start(bf16[256,256]{1,0:T(8,128)(2,1)} %reshape.393) | copy-start | bytes 393220
  187.6 2.5 copy-start.23
  (24 other events, 30.0 us)
Sparse Core Ops, SparseCore 0:
  141.7 169.1 all-reduce.4
  313.4 77.4 all-reduce.6
